TPU v7x, 32 devices: a whole 2x2x4 slice. The times are simulated.
32 devices in a mesh: section: 2 (over y), design: 8 (over z, x), batch: 2 (over core).
Axes of the slice: x: 2, y: 2, z: 4, core: 2. Of those that a mesh axis runs over, the one named last changes fastest.
Arguments:
- samples: float32 [64, 4096], replicated, may hold values from -6 to 6
- order: int32 [4096], P('batch'), may hold values from 0 to 4095, each once
- design_points: bfloat16 [2, 64, 16384], P('section', None, 'design'), may hold values from -6 to 6
- weights: bfloat16 [2, 64, 16384], P('section', None, 'design'), may hold values from -2 to 2
- length_sq: float32 [2, 64], replicated, may hold values from 8 to 128
Outputs:
- moments: float32 [2, 4, 64, 1024], P('section', None, None, ('batch', 'design'))
Inputs may be any that keep to these rules, and one draw needn't show every extreme that they name: `order`: each sample index appears exactly once.
All inputs are finite; a program needn't handle non-finite values.
Results may differ from a plain program's by a relative error of at most 0.0037.
Values may be sent and summed in bfloat16 or wider, within the bound.
A program may use at most 64 MiB of HBM per device.

v0:
```python
import jax
import jax.numpy as jnp
from jax import lax
from jax.sharding import PartitionSpec as P

MICRO = 512


def passed_along(block, axis, distance):
    devices = range(lax.axis_size(axis))
    route = [(i - distance, i) for i in devices if i - distance in devices]
    return lax.ppermute(block, axis, route)


def local_sum(mean_in, var_in, points, squares, weight_rows, lengths):
    denom = lengths[:, None] + 2.0 * var_in
    offset = jnp.sum(mean_in * mean_in / denom, axis=0)
    log_scale = -0.5 * jnp.sum(jnp.log(1.0 + 2.0 * var_in / lengths[:, None]), axis=0)
    scaled = (mean_in / denom).astype(jnp.bfloat16)
    inverse = (1.0 / denom).astype(jnp.bfloat16)
    cross = lax.dot_general(
        scaled, points, (((0,), (0,)), ((), ())), preferred_element_type=jnp.float32
    )
    quad = lax.dot_general(
        inverse, squares, (((0,), (0,)), ((), ())), preferred_element_type=jnp.float32
    )
    kernel = jnp.exp(log_scale[:, None] - offset[:, None] + 2.0 * cross - quad).astype(jnp.bfloat16)
    return lax.dot_general(
        weight_rows, kernel, (((1,), (1,)), ((), ())), preferred_element_type=jnp.float32
    )


def square_of(points):
    wide = points.astype(jnp.float32)
    return (wide * wide).astype(jnp.bfloat16)


def shards(samples, order, design_points, weights, length_sq):
    section_index = lax.axis_index("section")
    is_first = section_index == 0
    points = design_points[0]
    weight_rows = weights[0]
    lengths = jnp.where(is_first, length_sq[0], length_sq[1])
    squares = square_of(points)
    feat = points.shape[0]
    half = feat // 2
    count = order.shape[0] // MICRO
    share = MICRO // lax.axis_size("design")
    column = lax.axis_index("design") * share

    def pick(turn):
        indices = order[turn * MICRO : (turn + 1) * MICRO]
        return jnp.take(samples, indices, axis=1)

    received = jnp.zeros((feat, MICRO), jnp.float32)
    zeros_rest = jnp.zeros((feat - half, MICRO), jnp.float32)
    firsts = []
    seconds = []
    for turn in range(count + 1):
        current = pick(min(turn, count - 1))
        earlier = pick(max(turn - 1, 0))
        moments_in = received
        later_mean = jnp.concatenate([moments_in[:half], earlier[half:]], axis=0)
        later_var = jnp.concatenate([moments_in[half:], zeros_rest], axis=0)
        mean_in = jnp.where(is_first, current, later_mean)
        var_in = jnp.where(is_first, 0.0, later_var)
        partial_sum = local_sum(mean_in, var_in, points, squares, weight_rows, lengths)
        summed = lax.psum(partial_sum, "design")
        layer_out = jnp.where(
            is_first,
            jnp.concatenate([summed[:half], jax.nn.softplus(summed[half:])], axis=0),
            summed,
        )
        received = passed_along(layer_out, "section", 1)
        block = lax.dynamic_slice_in_dim(layer_out, column, share, 1)
        if turn < count:
            firsts.append(block)
        if turn > 0:
            seconds.append(block)
    result = jnp.where(is_first, jnp.stack(firsts, axis=0), jnp.stack(seconds, axis=0))
    return result[None]


def solution(mesh):
    placed = (P(), P("batch"), P("section", None, "design"), P("section", None, "design"), P())
    return jax.shard_map(
        shards,
        mesh=mesh,
        in_specs=placed,
        out_specs=P("section", None, None, ("batch", "design")),
        check_vma=False,
    )
```

profile of v0, /device:TPU:0, one launch (start us, length us, event | category | flops | bytes accessed | tf_op | source)
XLA Modules:
  0.0 447.8 jit_solution(6106497824247773900)
XLA Ops:
  9.5 1.8 copy.6
  11.3 1.0 gather_fusion
  12.6 2.7 fusion.23
  16.1 4.4 fusion.9
  20.5 73.3 %all-reduce.11.cloned.1.call-done = f32[64,512]{1,0:T(8,128)} async-done(((f32[64,512]{1,0:T(8,128)}), f32[64,512]{1,0:T(8,128)}) %all-reduce.11.cloned.1.call-update) | async-done | bytes 131088 | tf_op jit(solution)/shard_map/psum | solution.py:68
  93.8 0.9 fusion.144
  94.8 4.3 collective-permute-start
  99.1 1.0 gather_fusion.1
  100.3 1.3 collective-permute-done
  101.7 2.7 fusion.21
  104.5 4.4 fusion.8
  109.0 70.6 %all-reduce.13.cloned.1.call-done = f32[64,512]{1,0:T(8,128)} async-done(((f32[64,512]{1,0:T(8,128)}), f32[64,512]{1,0:T(8,128)}) %all-reduce.13.cloned.1.call-update) | async-done | bytes 131088 | tf_op jit(solution)/shard_map/psum | solution.py:68
  179.6 0.9 fusion.142
  180.6 4.9 %collective-permute-start.1 = (f32[64,512]{1,0:T(8,128)S(1)}, f32[64,512]{1,0:T(8,128)}, u32[]{:S(2)}, u32[]{:S(2)}) collective-permute-start(f32[64,512]{1,0:T(8,128)S(1)} %maximum_select_fusion.2), channel_id=1, source_target_pairs={{0,16},{1,17},{2,18},{3,19},{4,20},{5,21},{6,22},{7,23},{8,24},{9,... | collective-permute-start | bytes 393224 | tf_op jit(solution)/shard_map/ppermute | solution.py:12
  185.5 1.0 gather_fusion.2
  187.3 0.9 fusion.141
  188.4 2.7 fusion.19
  191.1 4.4 fusion.7
  195.6 70.7 %all-reduce.15.cloned.1.call-done = f32[64,512]{1,0:T(8,128)} async-done(((f32[64,512]{1,0:T(8,128)}), f32[64,512]{1,0:T(8,128)}) %all-reduce.15.cloned.1.call-update) | async-done | bytes 131088 | tf_op jit(solution)/shard_map/psum | solution.py:68
  266.3 0.9 fusion.140
  267.3 4.9 %collective-permute-start.2 = (f32[64,512]{1,0:T(8,128)S(1)}, f32[64,512]{1,0:T(8,128)}, u32[]{:S(2)}, u32[]{:S(2)}) collective-permute-start(f32[64,512]{1,0:T(8,128)S(1)} %maximum_select_fusion.4), channel_id=1, source_target_pairs={{0,16},{1,17},{2,18},{3,19},{4,20},{5,21},{6,22},{7,23},{8,24},{9,... | collective-permute-start | bytes 393224 | tf_op jit(solution)/shard_map/ppermute | solution.py:12
  272.2 1.0 gather_fusion.3
  275.1 2.7 fusion.17
  277.8 4.4 fusion.6
  282.3 70.8 %all-reduce.17.cloned.1.call-done = f32[64,512]{1,0:T(8,128)} async-done(((f32[64,512]{1,0:T(8,128)}), f32[64,512]{1,0:T(8,128)}) %all-reduce.17.cloned.1.call-update) | async-done | bytes 131088 | tf_op jit(solution)/shard_map/psum | solution.py:68
  353.1 0.9 fusion.138
  354.0 4.3 collective-permute-start.3
  358.5 2.3 collective-permute-done.3
  361.0 2.7 fusion.15
  363.7 4.4 fusion.5
  368.3 70.5 %all-reduce.19.cloned.1.call-done = f32[64,512]{1,0:T(8,128)} async-done(((f32[64,512]{1,0:T(8,128)}), f32[64,512]{1,0:T(8,128)}) %all-reduce.19.cloned.1.call-update) | async-done | bytes 131088 | tf_op jit(solution)/shard_map/psum | solution.py:68
  438.8 0.9 compare_select_fusion
  (54 shorter events, 8.6 us)
Async XLA Ops:
  6.5 9.5 %copy-start = (bf16[1,64,2048]{2,1,0:T(8,128)(2,1)S(1)}, bf16[1,64,2048]{2,1,0:T(8,128)(2,1)}, u32[]{:S(2)}) copy-start(bf16[1,64,2048]{2,1,0:T(8,128)(2,1)} %param.10) | copy-start | bytes 786436
  6.5 6.1 %copy-start.1 = (bf16[1,64,2048]{2,1,0:T(8,128)(2,1)S(1)}, bf16[1,64,2048]{2,1,0:T(8,128)(2,1)}, u32[]{:S(2)}) copy-start(bf16[1,64,2048]{2,1,0:T(8,128)(2,1)} %param.9) | copy-start | bytes 786436
  6.5 87.3 %all-reduce.11.cloned.1.call-start = ((), (), s32[]{:S(2)}) async-start(), calls=%async_computation | async-start | bytes 262144 | tf_op jit(solution)/shard_map/psum | solution.py:68
  20.5 159.1 %all-reduce.13.cloned.1.call-start = ((), (), s32[]{:S(2)}) async-start(), calls=%async_computation.1 | async-start | bytes 262144 | tf_op jit(solution)/shard_map/psum | solution.py:68
  94.8 6.8 %collective-permute-start = (f32[64,512]{1,0:T(8,128)S(1)}, f32[64,512]{1,0:T(8,128)S(1)}, u32[]{:S(2)}, u32[]{:S(2)}) collective-permute-start(f32[64,512]{1,0:T(8,128)S(1)} %maximum_select_fusion), channel_id=1, source_target_pairs={{0,16},{1,17},{2,18},{3,19},{4,20},{5,21},{6,22},{7,23},{8,24},{9,... | collective-permute-start | bytes 393224 | tf_op jit(solution)/shard_map/ppermute | solution.py:12
  108.9 157.4 %all-reduce.15.cloned.1.call-start = ((), (), s32[]{:S(2)}) async-start(), calls=%async_computation.2 | async-start | bytes 262144 | tf_op jit(solution)/shard_map/psum | solution.py:68
  180.6 6.8 %collective-permute-start.1 = (f32[64,512]{1,0:T(8,128)S(1)}, f32[64,512]{1,0:T(8,128)}, u32[]{:S(2)}, u32[]{:S(2)}) collective-permute-start(f32[64,512]{1,0:T(8,128)S(1)} %maximum_select_fusion.2), channel_id=1, source_target_pairs={{0,16},{1,17},{2,18},{3,19},{4,20},{5,21},{6,22},{7,23},{8,24},{9,... | collective-permute-start | bytes 393224 | tf_op jit(solution)/shard_map/ppermute | solution.py:12
  195.5 157.5 %all-reduce.17.cloned.1.call-start = ((), (), s32[]{:S(2)}) async-start(), calls=%async_computation.3 | async-start | bytes 262144 | tf_op jit(solution)/shard_map/psum | solution.py:68
  267.3 6.8 %collective-permute-start.2 = (f32[64,512]{1,0:T(8,128)S(1)}, f32[64,512]{1,0:T(8,128)}, u32[]{:S(2)}, u32[]{:S(2)}) collective-permute-start(f32[64,512]{1,0:T(8,128)S(1)} %maximum_select_fusion.4), channel_id=1, source_target_pairs={{0,16},{1,17},{2,18},{3,19},{4,20},{5,21},{6,22},{7,23},{8,24},{9,... | collective-permute-start | bytes 393224 | tf_op jit(solution)/shard_map/ppermute | solution.py:12
  282.3 156.6 %all-reduce.19.cloned.1.call-start = ((), (), s32[]{:S(2)}) async-start(), calls=%async_computation.4 | async-start | bytes 262144 | tf_op jit(solution)/shard_map/psum | solution.py:68
  354.0 6.8 %collective-permute-start.3 = (f32[64,512]{1,0:T(8,128)S(1)}, f32[64,512]{1,0:T(8,128)S(1)}, u32[]{:S(2)}, u32[]{:S(2)}) collective-permute-start(f32[64,512]{1,0:T(8,128)S(1)} %maximum_select_fusion.6), channel_id=1, source_target_pairs={{0,16},{1,17},{2,18},{3,19},{4,20},{5,21},{6,22},{7,23},{8,24},{9,... | collective-permute-start | bytes 393224 | tf_op jit(solution)/shard_map/ppermute | solution.py:12
Sparse Core Ops, SparseCore 0:
  20.6 73.1 all-reduce.10
  109.0 70.5 all-reduce.12
  195.7 70.6 all-reduce.14
  282.4 70.6 all-reduce.16
  368.3 70.5 all-reduce.18
where the time goes:
time: 449 us; the launch traced here: 448 us
  waiting for transfers between devices  361 us (80%)
  matrix products  35.7 us (8%)
  starting transfers between devices  18.6 us (4%)
  between operations  14 us (3%)
  other arithmetic  9.83 us (2%)
  local copies, waits for them, and re-layouts  8.53 us (2%)
    psum x5, waiting for transfers between devices, shards(): summed = lax.psum(partial_sum, 'design')  356 us
    dot_general x5, matrix products, local_sum(): lax.dot_general(weight_rows, kernel, (((1,), (1,)), ((), ())), preferred_...  22.1 us
    ppermute x4, starting transfers between devices, passed_along(): return lax.ppermute(block, axis, route)  18.4 us
    dot_general x5, matrix products, local_sum(): lax.dot_general(scaled, points, (((0,), (0,)), ((), ())), preferred_eleme...  13.6 us
  transfers between devices with their start and end apart: 9, of which 9 were waited for; matrix products, arithmetic and copies ran while one was open for 1% of the time, Pallas kernels for 0%

commit v1 on v0

--- a/solution.py
+++ b/solution.py
@@ -65,7 +65,9 @@
         mean_in = jnp.where(is_first, current, later_mean)
         var_in = jnp.where(is_first, 0.0, later_var)
         partial_sum = local_sum(mean_in, var_in, points, squares, weight_rows, lengths)
-        summed = lax.psum(partial_sum, "design")
+        summed = partial_sum
+        for hop in (1, 2, 4):
+            summed = summed + lax.ppermute(summed, "design", [(dev, dev ^ hop) for dev in range(8)])
         layer_out = jnp.where(
             is_first,
             jnp.concatenate([summed[:half], jax.nn.softplus(summed[half:])], axis=0),

time: 449 us -> 159 us (0.35)
  waiting for transfers between devices: 361 us -> 71.6 us
  starting transfers between devices: 18.6 us -> 39.3 us
  between operations: 14 us -> 1 us
  other arithmetic: 9.83 us -> 4.97 us
    psum x5 -> x0, waiting for transfers between devices: 356 us -> none  [shards(): summed = lax.psum(partial_sum, 'design')]
    ppermute x0 -> x15, waiting for transfers between devices: none -> 66.6 us  [shards(): lax.ppermute(summed, 'design', [(dev, dev ^ hop) for dev in range(8)])]
    ppermute x0 -> x15, starting transfers between devices: none -> 20.9 us  [shards(): lax.ppermute(summed, 'design', [(dev, dev ^ hop) for dev in range(8)])]
  transfers between devices with their start and end apart: 9 -> 19, of which waited for: 9 -> 19; matrix products, arithmetic and copies ran while one was open for 1% -> 2% of each run, Pallas kernels for 0% -> 0%
where the time goes in v1:
time: 159 us; the launch traced here: 158 us
  waiting for transfers between devices  71.6 us (45%)
  starting transfers between devices  39.3 us (25%)
  matrix products  32.5 us (20%)
  local copies, waits for them, and re-layouts  8.53 us (5%)
  other arithmetic  4.97 us (3%)
    ppermute x15, waiting for transfers between devices, shards(): lax.ppermute(summed, 'design', [(dev, dev ^ hop) for dev in range(8)])  66.6 us
    ppermute x15, starting transfers between devices, shards(): lax.ppermute(summed, 'design', [(dev, dev ^ hop) for dev in range(8)])  20.9 us
    dot_general x5, matrix products, local_sum(): lax.dot_general(weight_rows, kernel, (((1,), (1,)), ((), ())), preferred_...  18.8 us
    ppermute x4, starting transfers between devices, passed_along(): return lax.ppermute(block, axis, route)  18.4 us
    dot_general x5, matrix products, local_sum(): lax.dot_general(scaled, points, (((0,), (0,)), ((), ())), preferred_eleme...  13.8 us
    ppermute x4, waiting for transfers between devices, passed_along(): return lax.ppermute(block, axis, route)  5 us
    gather x8, local copies, waits for them, and re-layouts, pick(): return jnp.take(samples, indices, axis=1)  4.58 us
  transfers between devices with their start and end apart: 19, of which 19 were waited for; matrix products, arithmetic and copies ran while one was open for 2% of the time, Pallas kernels for 0%

profile of v1, /device:TPU:0, one launch (start us, length us, event | category | flops | bytes accessed | tf_op | source)
XLA Modules:
  0.0 157.9 jit_solution(5990265104182746584)
XLA Ops:
  6.1 2.8 %fusion.23 = f32[512,2048]{1,0:T(8,128)} fusion(bf16[1,64,2048]{2,1,0:T(8,128)(2,1)S(1)} %copy-done.1, f32[64,512]{1,0:T(8,128)S(1)} %select_bitcast_fusion.3, f32[32,512]{1,0:T(8,128)S(1)} %slice.127, f32[64]{0:T(128)S(1)} %get-tuple-element.18, pred[]{:T(512)S(6)} %eq.3), kind=kOutput, calls=%fused_computation.33 | convolution fusion | flops 134316032 | bytes 4653313 | tf_op jit(solution)/shard_map/dot_general | solution.py:21
  9.5 3.7 %fusion.9 = f32[64,512]{1,0:T(8,128)S(1)} fusion(f32[512,2048]{1,0:T(8,128)} %fusion.23, f32[512]{0:T(512)S(1)} %broadcast_subtract_fusion, bf16[1,64,2048]{2,1,0:T(8,128)(2,1)S(1)} %copy-done, bf16[1,64,2048]{2,1,0:T(8,128)(2,1)S(1)} %copy-done.1, bf16[64]{0:T(256)(128)(2,1)S(1)} %get-tuple-element.17), kind=kOutput, calls=%fused_computation.18 | convolution fusion | flops 273022976 | bytes 4851840 | tf_op jit(solution)/shard_map/dot_general | solution.py:28
  13.3 3.0 %collective-permute-start = (f32[64,512]{1,0:T(8,128)S(1)}, f32[64,512]{1,0:T(8,128)S(1)}, u32[]{:S(2)}, u32[]{:S(2)}) collective-permute-start(f32[64,512]{1,0:T(8,128)S(1)} %fusion.9), channel_id=1, source_target_pairs={{0,2},{2,0},{4,6},{6,4},{8,10},{10,8},{12,14},{14,12},{1,3},{3,1},... | collective-permute-start | bytes 393224 | tf_op jit(solution)/shard_map/ppermute | solution.py:70
  16.3 3.5 %collective-permute-done = f32[64,512]{1,0:T(8,128)S(1)} collective-permute-done((f32[64,512]{1,0:T(8,128)S(1)}, f32[64,512]{1,0:T(8,128)S(1)}, u32[]{:S(2)}, u32[]{:S(2)}) %collective-permute-start) | collective-permute-done | bytes 131104 | tf_op jit(solution)/shard_map/ppermute | solution.py:70
  21.7 3.1 %collective-permute-done.1 = f32[64,512]{1,0:T(8,128)S(1)} collective-permute-done((f32[64,512]{1,0:T(8,128)S(1)}, f32[64,512]{1,0:T(8,128)S(1)}, u32[]{:S(2)}, u32[]{:S(2)}) %collective-permute-start.1) | collective-permute-done | bytes 131104 | tf_op jit(solution)/shard_map/ppermute | solution.py:70
  24.9 2.9 %collective-permute-start.2 = (f32[64,512]{1,0:T(8,128)S(1)}, f32[64,512]{1,0:T(8,128)S(1)}, u32[]{:S(2)}, u32[]{:S(2)}) collective-permute-start(f32[64,512]{1,0:T(8,128)S(1)} %add.173), channel_id=1, source_target_pairs={{0,8},{2,10},{4,12},{6,14},{8,0},{10,2},{12,4},{14,6},{1,9},{3,11}... | collective-permute-start | bytes 393224 | tf_op jit(solution)/shard_map/ppermute | solution.py:70
  27.8 4.4 %collective-permute-done.2 = f32[64,512]{1,0:T(8,128)S(1)} collective-permute-done((f32[64,512]{1,0:T(8,128)S(1)}, f32[64,512]{1,0:T(8,128)S(1)}, u32[]{:S(2)}, u32[]{:S(2)}) %collective-permute-start.2) | collective-permute-done | bytes 131104 | tf_op jit(solution)/shard_map/ppermute | solution.py:70
  32.3 3.7 %collective-permute-start.3 = (f32[64,512]{1,0:T(8,128)S(1)}, f32[64,512]{1,0:T(8,128)S(1)}, u32[]{:S(2)}, u32[]{:S(2)}) collective-permute-start(f32[64,512]{1,0:T(8,128)S(1)} %maximum_select_fusion), channel_id=1, source_target_pairs={{0,16},{1,17},{2,18},{3,19},{4,20},{5,21},{6,22},{7,23},{8,24},{9,... | collective-permute-start | bytes 393224 | tf_op jit(solution)/shard_map/ppermute | solution.py:12
  38.7 2.8 %fusion.21 = f32[512,2048]{1,0:T(8,128)} fusion(bf16[1,64,2048]{2,1,0:T(8,128)(2,1)S(1)} %copy-done.1, f32[32,512]{1,0:T(8,128)S(1)} %get-tuple-element.34, f32[64]{0:T(128)S(1)} %get-tuple-element.18, pred[]{:T(512)S(6)} %eq.3, f32[64,512]{1,0:T(8,128)S(1)} %get-tuple-element.16, f32[32,512]{1,0:T(8,128)S(1)} %slice.127, f32[32,512]{1,0:T(8,128)S(1)} %get-tuple-element.33), kind=kOutput, calls=%fused_computation.31 | convolution fusion | flops 134447104 | bytes 4784385 | tf_op jit(solution)/shard_map/dot_general | solution.py:21
  41.4 3.8 %fusion.8 = f32[64,512]{1,0:T(8,128)S(1)} fusion(f32[512,2048]{1,0:T(8,128)} %fusion.21, f32[512]{0:T(512)S(1)} %multiply_subtract_fusion.3, bf16[1,64,2048]{2,1,0:T(8,128)(2,1)S(1)} %copy-done, bf16[1,64,2048]{2,1,0:T(8,128)(2,1)S(1)} %copy-done.1, f32[32,512]{1,0:T(8,128)S(1)} %get-tuple-element.34, f32[64]{0:T(128)S(1)} %get-tuple-element.18, pred[]{:T(512)S(6)} %eq.3), kind=kOutput, calls=%fused_computation.17 | convolution fusion | flops 273186816 | bytes 4917505 | tf_op jit(solution)/shard_map/dot_general | solution.py:28
  46.7 3.5 %collective-permute-done.4 = f32[64,512]{1,0:T(8,128)S(1)} collective-permute-done((f32[64,512]{1,0:T(8,128)S(1)}, f32[64,512]{1,0:T(8,128)S(1)}, u32[]{:S(2)}, u32[]{:S(2)}) %collective-permute-start.4) | collective-permute-done | bytes 131104 | tf_op jit(solution)/shard_map/ppermute | solution.py:70
  51.0 4.7 %collective-permute-done.5 = f32[64,512]{1,0:T(8,128)S(1)} collective-permute-done((f32[64,512]{1,0:T(8,128)S(1)}, f32[64,512]{1,0:T(8,128)S(1)}, u32[]{:S(2)}, u32[]{:S(2)}) %collective-permute-start.5) | collective-permute-done | bytes 131104 | tf_op jit(solution)/shard_map/ppermute | solution.py:70
  57.8 5.2 %collective-permute-done.6 = f32[64,512]{1,0:T(8,128)S(1)} collective-permute-done((f32[64,512]{1,0:T(8,128)S(1)}, f32[64,512]{1,0:T(8,128)S(1)}, u32[]{:S(2)}, u32[]{:S(2)}) %collective-permute-start.6) | collective-permute-done | bytes 131104 | tf_op jit(solution)/shard_map/ppermute | solution.py:70
  63.2 5.0 %collective-permute-start.7 = (f32[64,512]{1,0:T(8,128)S(1)}, f32[64,512]{1,0:T(8,128)}, u32[]{:S(2)}, u32[]{:S(2)}) collective-permute-start(f32[64,512]{1,0:T(8,128)S(1)} %maximum_select_fusion.2), channel_id=1, source_target_pairs={{0,16},{1,17},{2,18},{3,19},{4,20},{5,21},{6,22},{7,23},{8,24},{9,... | collective-permute-start | bytes 393224 | tf_op jit(solution)/shard_map/ppermute | solution.py:12
  71.0 2.8 %fusion.19 = f32[512,2048]{1,0:T(8,128)} fusion(bf16[1,64,2048]{2,1,0:T(8,128)(2,1)S(1)} %copy-done.1, f32[32,512]{1,0:T(8,128)S(1)} %get-tuple-element.30, f32[64]{0:T(128)S(1)} %get-tuple-element.18, pred[]{:T(512)S(6)} %eq.3, f32[64,512]{1,0:T(8,128)S(1)} %get-tuple-element.15, f32[32,512]{1,0:T(8,128)S(1)} %slice.136, f32[32,512]{1,0:T(8,128)S(1)} %get-tuple-element.29), kind=kOutput, calls=%fused_computation.29 | convolution fusion | flops 134447104 | bytes 4784385 | tf_op jit(solution)/shard_map/dot_general | solution.py:21
  73.8 3.8 %fusion.7 = f32[64,512]{1,0:T(8,128)S(1)} fusion(f32[512,2048]{1,0:T(8,128)} %fusion.19, f32[512]{0:T(512)S(1)} %multiply_subtract_fusion.2, bf16[1,64,2048]{2,1,0:T(8,128)(2,1)S(1)} %copy-done, bf16[1,64,2048]{2,1,0:T(8,128)(2,1)S(1)} %copy-done.1, f32[32,512]{1,0:T(8,128)S(1)} %get-tuple-element.30, f32[64]{0:T(128)S(1)} %get-tuple-element.18, pred[]{:T(512)S(6)} %eq.3), kind=kOutput, calls=%fused_computation.16 | convolution fusion | flops 273186816 | bytes 4917505 | tf_op jit(solution)/shard_map/dot_general | solution.py:28
  79.1 3.4 %collective-permute-done.8 = f32[64,512]{1,0:T(8,128)S(1)} collective-permute-done((f32[64,512]{1,0:T(8,128)S(1)}, f32[64,512]{1,0:T(8,128)S(1)}, u32[]{:S(2)}, u32[]{:S(2)}) %collective-permute-start.8) | collective-permute-done | bytes 131104 | tf_op jit(solution)/shard_map/ppermute | solution.py:70
  82.9 4.7 %collective-permute-done.9 = f32[64,512]{1,0:T(8,128)S(1)} collective-permute-done((f32[64,512]{1,0:T(8,128)S(1)}, f32[64,512]{1,0:T(8,128)S(1)}, u32[]{:S(2)}, u32[]{:S(2)}) %collective-permute-start.9) | collective-permute-done | bytes 131104 | tf_op jit(solution)/shard_map/ppermute | solution.py:70
  89.2 5.8 %collective-permute-done.10 = f32[64,512]{1,0:T(8,128)S(1)} collective-permute-done((f32[64,512]{1,0:T(8,128)S(1)}, f32[64,512]{1,0:T(8,128)S(1)}, u32[]{:S(2)}, u32[]{:S(2)}) %collective-permute-start.10) | collective-permute-done | bytes 131104 | tf_op jit(solution)/shard_map/ppermute | solution.py:70
  95.1 5.1 %collective-permute-start.11 = (f32[64,512]{1,0:T(8,128)S(1)}, f32[64,512]{1,0:T(8,128)}, u32[]{:S(2)}, u32[]{:S(2)}) collective-permute-start(f32[64,512]{1,0:T(8,128)S(1)} %maximum_select_fusion.4), channel_id=1, source_target_pairs={{0,16},{1,17},{2,18},{3,19},{4,20},{5,21},{6,22},{7,23},{8,24},{9,... | collective-permute-start | bytes 393224 | tf_op jit(solution)/shard_map/ppermute | solution.py:12
  103.1 2.8 %fusion.17 = f32[512,2048]{1,0:T(8,128)} fusion(bf16[1,64,2048]{2,1,0:T(8,128)(2,1)S(1)} %copy-done.1, f32[32,512]{1,0:T(8,128)S(1)} %get-tuple-element.26, f32[64]{0:T(128)S(1)} %get-tuple-element.18, pred[]{:T(512)S(6)} %eq.3, f32[64,512]{1,0:T(8,128)S(1)} %get-tuple-element.14, f32[32,512]{1,0:T(8,128)S(1)} %slice.141, f32[32,512]{1,0:T(8,128)S(1)} %get-tuple-element.25), kind=kOutput, calls=%fused_computation.27 | convolution fusion | flops 134447104 | bytes 4784385 | tf_op jit(solution)/shard_map/dot_general | solution.py:21
  105.8 3.8 %fusion.6 = f32[64,512]{1,0:T(8,128)S(1)} fusion(f32[512,2048]{1,0:T(8,128)} %fusion.17, f32[512]{0:T(512)S(1)} %multiply_subtract_fusion.1, bf16[1,64,2048]{2,1,0:T(8,128)(2,1)S(1)} %copy-done, bf16[1,64,2048]{2,1,0:T(8,128)(2,1)S(1)} %copy-done.1, f32[32,512]{1,0:T(8,128)S(1)} %get-tuple-element.26, f32[64]{0:T(128)S(1)} %get-tuple-element.18, pred[]{:T(512)S(6)} %eq.3), kind=kOutput, calls=%fused_computation.15 | convolution fusion | flops 273186816 | bytes 4917505 | tf_op jit(solution)/shard_map/dot_general | solution.py:28
  111.1 3.5 %collective-permute-done.12 = f32[64,512]{1,0:T(8,128)S(1)} collective-permute-done((f32[64,512]{1,0:T(8,128)S(1)}, f32[64,512]{1,0:T(8,128)S(1)}, u32[]{:S(2)}, u32[]{:S(2)}) %collective-permute-start.12) | collective-permute-done | bytes 131104 | tf_op jit(solution)/shard_map/ppermute | solution.py:70
  114.7 5.0 %collective-permute-done.13 = f32[64,512]{1,0:T(8,128)S(1)} collective-permute-done((f32[64,512]{1,0:T(8,128)S(1)}, f32[64,512]{1,0:T(8,128)S(1)}, u32[]{:S(2)}, u32[]{:S(2)}) %collective-permute-start.13) | collective-permute-done | bytes 131104 | tf_op jit(solution)/shard_map/ppermute | solution.py:70
  120.7 5.8 %collective-permute-done.14 = f32[64,512]{1,0:T(8,128)S(1)} collective-permute-done((f32[64,512]{1,0:T(8,128)S(1)}, f32[64,512]{1,0:T(8,128)S(1)}, u32[]{:S(2)}, u32[]{:S(2)}) %collective-permute-start.14) | collective-permute-done | bytes 131104 | tf_op jit(solution)/shard_map/ppermute | solution.py:70
  126.6 4.6 %collective-permute-start.15 = (f32[64,512]{1,0:T(8,128)S(1)}, f32[64,512]{1,0:T(8,128)S(1)}, u32[]{:S(2)}, u32[]{:S(2)}) collective-permute-start(f32[64,512]{1,0:T(8,128)S(1)} %maximum_select_fusion.6), channel_id=1, source_target_pairs={{0,16},{1,17},{2,18},{3,19},{4,20},{5,21},{6,22},{7,23},{8,24},{9,... | collective-permute-start | bytes 393224 | tf_op jit(solution)/shard_map/ppermute | solution.py:12
  131.2 2.3 %collective-permute-done.15 = f32[64,512]{1,0:T(8,128)S(1)} collective-permute-done((f32[64,512]{1,0:T(8,128)S(1)}, f32[64,512]{1,0:T(8,128)S(1)}, u32[]{:S(2)}, u32[]{:S(2)}) %collective-permute-start.15) | collective-permute-done | bytes 131104 | tf_op jit(solution)/shard_map/ppermute | solution.py:12
  133.7 2.8 %fusion.15 = f32[512,2048]{1,0:T(8,128)} fusion(bf16[1,64,2048]{2,1,0:T(8,128)(2,1)S(1)} %copy-done.1, f32[32,512]{1,0:T(8,128)S(1)} %get-tuple-element.22, f32[64]{0:T(128)S(1)} %get-tuple-element.18, pred[]{:T(512)S(6)} %eq.3, f32[64,512]{1,0:T(8,128)S(1)} %get-tuple-element.14, f32[32,512]{1,0:T(8,128)S(1)} %slice.146, f32[32,512]{1,0:T(8,128)S(1)} %get-tuple-element.21), kind=kOutput, calls=%fused_computation.25 | convolution fusion | flops 134447104 | bytes 4784385 | tf_op jit(solution)/shard_map/dot_general | solution.py:21
  136.4 3.8 %fusion.5 = f32[64,512]{1,0:T(8,128)S(1)} fusion(f32[512,2048]{1,0:T(8,128)} %fusion.15, f32[512]{0:T(512)S(1)} %multiply_subtract_fusion, bf16[1,64,2048]{2,1,0:T(8,128)(2,1)S(1)} %copy-done, bf16[1,64,2048]{2,1,0:T(8,128)(2,1)S(1)} %copy-done.1, f32[32,512]{1,0:T(8,128)S(1)} %get-tuple-element.22, f32[64]{0:T(128)S(1)} %get-tuple-element.18, pred[]{:T(512)S(6)} %eq.3), kind=kOutput, calls=%fused_computation.14 | convolution fusion | flops 273186816 | bytes 4917505 | tf_op jit(solution)/shard_map/dot_general | solution.py:28
  141.8 3.5 %collective-permute-done.16 = f32[64,512]{1,0:T(8,128)S(1)} collective-permute-done((f32[64,512]{1,0:T(8,128)S(1)}, f32[64,512]{1,0:T(8,128)S(1)}, u32[]{:S(2)}, u32[]{:S(2)}) %collective-permute-start.16) | collective-permute-done | bytes 131104 | tf_op jit(solution)/shard_map/ppermute | solution.py:70
  145.5 4.8 %collective-permute-done.17 = f32[64,512]{1,0:T(8,128)S(1)} collective-permute-done((f32[64,512]{1,0:T(8,128)S(1)}, f32[64,512]{1,0:T(8,128)S(1)}, u32[]{:S(2)}, u32[]{:S(2)}) %collective-permute-start.17) | collective-permute-done | bytes 131104 | tf_op jit(solution)/shard_map/ppermute | solution.py:70
  151.4 5.7 %collective-permute-done.18 = f32[64,512]{1,0:T(8,128)S(1)} collective-permute-done((f32[64,512]{1,0:T(8,128)S(1)}, f32[64,512]{1,0:T(8,128)S(1)}, u32[]{:S(2)}, u32[]{:S(2)}) %collective-permute-start.18) | collective-permute-done | bytes 131104 | tf_op jit(solution)/shard_map/ppermute | solution.py:70
  (84 shorter events, 31.1 us)
Async XLA Ops:
  0.0 9.5 %copy-start = (bf16[1,64,2048]{2,1,0:T(8,128)(2,1)S(1)}, bf16[1,64,2048]{2,1,0:T(8,128)(2,1)}, u32[]{:S(2)}) copy-start(bf16[1,64,2048]{2,1,0:T(8,128)(2,1)} %param.10) | copy-start | bytes 786436
  0.0 6.1 %copy-start.1 = (bf16[1,64,2048]{2,1,0:T(8,128)(2,1)S(1)}, bf16[1,64,2048]{2,1,0:T(8,128)(2,1)}, u32[]{:S(2)}) copy-start(bf16[1,64,2048]{2,1,0:T(8,128)(2,1)} %param.9) | copy-start | bytes 786436
  13.3 6.5 %collective-permute-start = (f32[64,512]{1,0:T(8,128)S(1)}, f32[64,512]{1,0:T(8,128)S(1)}, u32[]{:S(2)}, u32[]{:S(2)}) collective-permute-start(f32[64,512]{1,0:T(8,128)S(1)} %fusion.9), channel_id=1, source_target_pairs={{0,2},{2,0},{4,6},{6,4},{8,10},{10,8},{12,14},{14,12},{1,3},{3,1},... | collective-permute-start | bytes 393224 | tf_op jit(solution)/shard_map/ppermute | solution.py:70
  19.8 5.0 %collective-permute-start.1 = (f32[64,512]{1,0:T(8,128)S(1)}, f32[64,512]{1,0:T(8,128)S(1)}, u32[]{:S(2)}, u32[]{:S(2)}) collective-permute-start(f32[64,512]{1,0:T(8,128)S(1)} %add.172), channel_id=1, source_target_pairs={{0,4},{2,6},{4,0},{6,2},{8,12},{10,14},{12,8},{14,10},{1,5},{3,7},... | collective-permute-start | bytes 393224 | tf_op jit(solution)/shard_map/ppermute | solution.py:70
  24.9 7.3 %collective-permute-start.2 = (f32[64,512]{1,0:T(8,128)S(1)}, f32[64,512]{1,0:T(8,128)S(1)}, u32[]{:S(2)}, u32[]{:S(2)}) collective-permute-start(f32[64,512]{1,0:T(8,128)S(1)} %add.173), channel_id=1, source_target_pairs={{0,8},{2,10},{4,12},{6,14},{8,0},{10,2},{12,4},{14,6},{1,9},{3,11}... | collective-permute-start | bytes 393224 | tf_op jit(solution)/shard_map/ppermute | solution.py:70
  32.3 6.2 %collective-permute-start.3 = (f32[64,512]{1,0:T(8,128)S(1)}, f32[64,512]{1,0:T(8,128)S(1)}, u32[]{:S(2)}, u32[]{:S(2)}) collective-permute-start(f32[64,512]{1,0:T(8,128)S(1)} %maximum_select_fusion), channel_id=1, source_target_pairs={{0,16},{1,17},{2,18},{3,19},{4,20},{5,21},{6,22},{7,23},{8,24},{9,... | collective-permute-start | bytes 393224 | tf_op jit(solution)/shard_map/ppermute | solution.py:12
  45.2 5.0 %collective-permute-start.4 = (f32[64,512]{1,0:T(8,128)S(1)}, f32[64,512]{1,0:T(8,128)S(1)}, u32[]{:S(2)}, u32[]{:S(2)}) collective-permute-start(f32[64,512]{1,0:T(8,128)S(1)} %fusion.8), channel_id=1, source_target_pairs={{0,2},{2,0},{4,6},{6,4},{8,10},{10,8},{12,14},{14,12},{1,3},{3,1},... | collective-permute-start | bytes 393224 | tf_op jit(solution)/shard_map/ppermute | solution.py:70
  50.2 5.5 %collective-permute-start.5 = (f32[64,512]{1,0:T(8,128)S(1)}, f32[64,512]{1,0:T(8,128)S(1)}, u32[]{:S(2)}, u32[]{:S(2)}) collective-permute-start(f32[64,512]{1,0:T(8,128)S(1)} %add.181), channel_id=1, source_target_pairs={{0,4},{2,6},{4,0},{6,2},{8,12},{10,14},{12,8},{14,10},{1,5},{3,7},... | collective-permute-start | bytes 393224 | tf_op jit(solution)/shard_map/ppermute | solution.py:70
  55.7 7.3 %collective-permute-start.6 = (f32[64,512]{1,0:T(8,128)S(1)}, f32[64,512]{1,0:T(8,128)S(1)}, u32[]{:S(2)}, u32[]{:S(2)}) collective-permute-start(f32[64,512]{1,0:T(8,128)S(1)} %add.182), channel_id=1, source_target_pairs={{0,8},{2,10},{4,12},{6,14},{8,0},{10,2},{12,4},{14,6},{1,9},{3,11}... | collective-permute-start | bytes 393224 | tf_op jit(solution)/shard_map/ppermute | solution.py:70
  63.2 6.9 %collective-permute-start.7 = (f32[64,512]{1,0:T(8,128)S(1)}, f32[64,512]{1,0:T(8,128)}, u32[]{:S(2)}, u32[]{:S(2)}) collective-permute-start(f32[64,512]{1,0:T(8,128)S(1)} %maximum_select_fusion.2), channel_id=1, source_target_pairs={{0,16},{1,17},{2,18},{3,19},{4,20},{5,21},{6,22},{7,23},{8,24},{9,... | collective-permute-start | bytes 393224 | tf_op jit(solution)/shard_map/ppermute | solution.py:12
  77.5 5.0 %collective-permute-start.8 = (f32[64,512]{1,0:T(8,128)S(1)}, f32[64,512]{1,0:T(8,128)S(1)}, u32[]{:S(2)}, u32[]{:S(2)}) collective-permute-start(f32[64,512]{1,0:T(8,128)S(1)} %fusion.7), channel_id=1, source_target_pairs={{0,2},{2,0},{4,6},{6,4},{8,10},{10,8},{12,14},{14,12},{1,3},{3,1},... | collective-permute-start | bytes 393224 | tf_op jit(solution)/shard_map/ppermute | solution.py:70
  82.6 5.0 %collective-permute-start.9 = (f32[64,512]{1,0:T(8,128)S(1)}, f32[64,512]{1,0:T(8,128)S(1)}, u32[]{:S(2)}, u32[]{:S(2)}) collective-permute-start(f32[64,512]{1,0:T(8,128)S(1)} %add.189), channel_id=1, source_target_pairs={{0,4},{2,6},{4,0},{6,2},{8,12},{10,14},{12,8},{14,10},{1,5},{3,7},... | collective-permute-start | bytes 393224 | tf_op jit(solution)/shard_map/ppermute | solution.py:70
  87.7 7.3 %collective-permute-start.10 = (f32[64,512]{1,0:T(8,128)S(1)}, f32[64,512]{1,0:T(8,128)S(1)}, u32[]{:S(2)}, u32[]{:S(2)}) collective-permute-start(f32[64,512]{1,0:T(8,128)S(1)} %add.190), channel_id=1, source_target_pairs={{0,8},{2,10},{4,12},{6,14},{8,0},{10,2},{12,4},{14,6},{1,9},{3,11}... | collective-permute-start | bytes 393224 | tf_op jit(solution)/shard_map/ppermute | solution.py:70
  95.1 7.0 %collective-permute-start.11 = (f32[64,512]{1,0:T(8,128)S(1)}, f32[64,512]{1,0:T(8,128)}, u32[]{:S(2)}, u32[]{:S(2)}) collective-permute-start(f32[64,512]{1,0:T(8,128)S(1)} %maximum_select_fusion.4), channel_id=1, source_target_pairs={{0,16},{1,17},{2,18},{3,19},{4,20},{5,21},{6,22},{7,23},{8,24},{9,... | collective-permute-start | bytes 393224 | tf_op jit(solution)/shard_map/ppermute | solution.py:12
  109.6 5.0 %collective-permute-start.12 = (f32[64,512]{1,0:T(8,128)S(1)}, f32[64,512]{1,0:T(8,128)S(1)}, u32[]{:S(2)}, u32[]{:S(2)}) collective-permute-start(f32[64,512]{1,0:T(8,128)S(1)} %fusion.6), channel_id=1, source_target_pairs={{0,2},{2,0},{4,6},{6,4},{8,10},{10,8},{12,14},{14,12},{1,3},{3,1},... | collective-permute-start | bytes 393224 | tf_op jit(solution)/shard_map/ppermute | solution.py:70
  114.6 5.0 %collective-permute-start.13 = (f32[64,512]{1,0:T(8,128)S(1)}, f32[64,512]{1,0:T(8,128)S(1)}, u32[]{:S(2)}, u32[]{:S(2)}) collective-permute-start(f32[64,512]{1,0:T(8,128)S(1)} %add.197), channel_id=1, source_target_pairs={{0,4},{2,6},{4,0},{6,2},{8,12},{10,14},{12,8},{14,10},{1,5},{3,7},... | collective-permute-start | bytes 393224 | tf_op jit(solution)/shard_map/ppermute | solution.py:70
  119.7 6.8 %collective-permute-start.14 = (f32[64,512]{1,0:T(8,128)S(1)}, f32[64,512]{1,0:T(8,128)S(1)}, u32[]{:S(2)}, u32[]{:S(2)}) collective-permute-start(f32[64,512]{1,0:T(8,128)S(1)} %add.198), channel_id=1, source_target_pairs={{0,8},{2,10},{4,12},{6,14},{8,0},{10,2},{12,4},{14,6},{1,9},{3,11}... | collective-permute-start | bytes 393224 | tf_op jit(solution)/shard_map/ppermute | solution.py:70
  126.6 7.0 %collective-permute-start.15 = (f32[64,512]{1,0:T(8,128)S(1)}, f32[64,512]{1,0:T(8,128)S(1)}, u32[]{:S(2)}, u32[]{:S(2)}) collective-permute-start(f32[64,512]{1,0:T(8,128)S(1)} %maximum_select_fusion.6), channel_id=1, source_target_pairs={{0,16},{1,17},{2,18},{3,19},{4,20},{5,21},{6,22},{7,23},{8,24},{9,... | collective-permute-start | bytes 393224 | tf_op jit(solution)/shard_map/ppermute | solution.py:12
  140.2 5.0 %collective-permute-start.16 = (f32[64,512]{1,0:T(8,128)S(1)}, f32[64,512]{1,0:T(8,128)S(1)}, u32[]{:S(2)}, u32[]{:S(2)}) collective-permute-start(f32[64,512]{1,0:T(8,128)S(1)} %fusion.5), channel_id=1, source_target_pairs={{0,2},{2,0},{4,6},{6,4},{8,10},{10,8},{12,14},{14,12},{1,3},{3,1},... | collective-permute-start | bytes 393224 | tf_op jit(solution)/shard_map/ppermute | solution.py:70
  145.3 5.0 %collective-permute-start.17 = (f32[64,512]{1,0:T(8,128)S(1)}, f32[64,512]{1,0:T(8,128)S(1)}, u32[]{:S(2)}, u32[]{:S(2)}) collective-permute-start(f32[64,512]{1,0:T(8,128)S(1)} %add.205), channel_id=1, source_target_pairs={{0,4},{2,6},{4,0},{6,2},{8,12},{10,14},{12,8},{14,10},{1,5},{3,7},... | collective-permute-start | bytes 393224 | tf_op jit(solution)/shard_map/ppermute | solution.py:70
  150.3 6.8 %collective-permute-start.18 = (f32[64,512]{1,0:T(8,128)S(1)}, f32[64,512]{1,0:T(8,128)S(1)}, u32[]{:S(2)}, u32[]{:S(2)}) collective-permute-start(f32[64,512]{1,0:T(8,128)S(1)} %add.206), channel_id=1, source_target_pairs={{0,8},{2,10},{4,12},{6,14},{8,0},{10,2},{12,4},{14,6},{1,9},{3,11}... | collective-permute-start | bytes 393224 | tf_op jit(solution)/shard_map/ppermute | solution.py:70
